TPU v7x, 32 devices: a whole 2x2x4 slice. The times are simulated.
32 devices in a mesh: groups: 2 (over y), blk: 4 (over z), probe: 2 (over x), sub: 2 (over core).
Axes of the slice: x: 2, y: 2, z: 4, core: 2. Of those that a mesh axis runs over, the one named last changes fastest.
Arguments:
- coords: float32 [3, 16384], P(None, ('groups', 'blk')), parts along dimension 1, may hold values from -4 to 4
- noise_var: float32 [16384], P(('groups', 'blk')), parts along dimension 0, may hold values from 0.5 to 2
- probe_signs: int32 [64, 16384], P('probe', ('groups', 'blk')), parts along dimension 1, may hold values from -1 to 1, as said below
- tile_rows: int32 [8, 2, 96], P(('groups', 'blk'), 'sub'), parts along dimension 0, may hold values from 0 to 15
- tile_cols: int32 [8, 2, 96], P(('groups', 'blk'), 'sub'), parts along dimension 0, may hold values from 0 to 31, as said below
- tile_count: int32 [8, 2], P(('groups', 'blk'), 'sub'), parts along dimension 0, may hold values from 24 to 96
Outputs:
- alphas: float32 [3, 128], P(None, ('groups', 'probe')), parts along dimension 1
- betas: float32 [3, 128], P(None, ('groups', 'probe')), parts along dimension 1
- last_basis: float32 [64, 16384], P('probe', ('groups', 'blk')), parts along dimension 1
- coord_grad: float32 [3, 16384], P(None, ('groups', 'blk')), parts along dimension 1
There are 2 independent parts, one for each index of `groups`. A program takes and returns all parts, laid end to end along the dimension named above; each array names one. Nothing has to cross between parts.
Inputs may be any that keep to these rules, and one draw needn't show every extreme that they name: `probe_signs`: every entry is -1 or 1. tile_cols minus tile_rows lies between 0 and 16 in every slot.
All inputs are finite; a program needn't handle non-finite values.
Results may differ from a plain program's by a relative error of at most 0.00025.
Values sent between devices are 32-bit elements; how exact they have to be, the bound alone decides.
A program may use at most 64 MiB of HBM per device.

v0:
```python
import functools
import math

import jax
import jax.numpy as jnp
from jax import lax
from jax.experimental import pallas as pl
from jax.experimental.pallas import tpu as pltpu
from jax.sharding import PartitionSpec as P

ITERS = 3
SIGNAL_VAR = 0.1
LENGTH_SQ = 2.0
TAPER_SQ = 16.0
WARP_GAIN = 0.4
EPSILON = 1e-06

F32 = jnp.float32
BF16 = jnp.bfloat16
BL = 128
SB = 16
HB = 8
WB = 5 * HB
OFFS = 2 * SB + 1
PAIRS = HB * (SB + 1)
UNROLL = 4
TINY = 1e-30
SCALE = math.sqrt(TAPER_SQ)
EXPO = -TAPER_SQ / (2.0 * LENGTH_SQ) / math.log(2.0)
SLOPE = TAPER_SQ / (2.0 * LENGTH_SQ)
BUILD_VMEM = 2**22
APPLY_VMEM = 4 * 2**20
GRAD_VMEM = 6 * 2**20
VMEM = pl.BlockSpec(memory_space=pltpu.VMEM)
SMEM = pl.BlockSpec(memory_space=pltpu.SMEM)
HBM = pl.BlockSpec(memory_space=pltpu.HBM)
MESH = pl.DeviceIdType.MESH


def sds(shape, dtype=F32):
    return jax.ShapeDtypeStruct(shape, dtype)


def peer_of(me, step, n, axis):
    to = lax.rem(me + step + n, n)
    return {axis: to // 2, "sub": lax.rem(to, 2)}


def greet(peers):
    barrier = pltpu.get_barrier_semaphore()
    for peer in peers:
        pl.semaphore_signal(barrier, inc=1, device_id=peer, device_id_type=MESH)
    return barrier


def remote(src, dst, send, recv, peer):
    return pltpu.make_async_remote_copy(
        src_ref=src, dst_ref=dst, send_sem=send, recv_sem=recv,
        device_id=peer, device_id_type=MESH,
    )


def ship(own_ref, win_ref, sems, up, down, twin):
    wsend, wrecv, fsend, frecv = sems
    half = lax.axis_index("sub")
    chunks = own_ref.shape[0] // 8
    rows = [pl.ds(8 * c, 8) for c in range(chunks)]
    outs = []
    for c in range(chunks):
        outs.append(remote(own_ref.at[rows[c]], win_ref.at[0, rows[c]], wsend.at[0, c], wrecv.at[0, c], up))
        outs.append(remote(own_ref.at[rows[c]], win_ref.at[4, rows[c]], wsend.at[1, c], wrecv.at[1, c], down))
    for copy in outs:
        copy.start()
    own = remote(own_ref, win_ref.at[1 + 2 * half], fsend.at[chunks], frecv.at[chunks], twin)
    own.start()

    def finish():
        hand = []
        for c in range(chunks):
            piece = win_ref.at[4 - 4 * half, rows[c]]
            remote(piece, piece, wsend.at[0, c], wrecv.at[1 - half, c], twin).wait_recv()
            copy = remote(piece, win_ref.at[3 - 2 * half, rows[c]], fsend.at[c], frecv.at[c], twin)
            copy.start()
            hand.append(copy)
        own.wait()
        for copy in outs:
            copy.wait_send()
        for c in range(chunks):
            other = win_ref.at[4 * half, rows[c]]
            remote(other, other, wsend.at[0, c], wrecv.at[half, c], twin).wait_recv()
        for copy in hand:
            copy.wait()

    return finish


def ship_sems(own):
    chunks = own.shape[0] // 8
    dma = pltpu.SemaphoreType.DMA
    return [dma((2, chunks)), dma((2, chunks)), dma((chunks + 1,)), dma((chunks + 1,))]


def entry_kernel(n, x_ref, r_ref, c_ref, t_ref, win_ref, rows_ref, cols_ref, tots_ref, send, recv, lsem):
    blk, half = lax.axis_index("blk"), lax.axis_index("sub")
    above, below = lax.rem(blk + 1, n), lax.rem(blk + n - 1, n)
    up = {"blk": above, "sub": half}
    down = {"blk": below, "sub": half}
    cross = {"blk": above, "sub": 1 - half}
    under = {"blk": below, "sub": 1 - half}
    twin = {"blk": blk, "sub": 1 - half}
    barrier = greet((up, down, cross, under, twin))
    lists = ((r_ref, rows_ref), (c_ref, cols_ref), (t_ref, tots_ref))
    local = [pltpu.make_async_copy(x_ref, win_ref.at[1], lsem.at[0])]
    for k, (src, dst) in enumerate(lists):
        local.append(pltpu.make_async_copy(src, dst.at[2], lsem.at[1 + k]))
    for copy in local:
        copy.start()
    pl.semaphore_wait(barrier, 5)
    copies = [
        remote(x_ref, win_ref.at[0], send.at[0], recv.at[0], up),
        remote(x_ref, win_ref.at[2], send.at[1], recv.at[1], down),
    ]
    for k, (src, dst) in enumerate(lists):
        for j, (slot, peer) in enumerate(((1, cross), (0, up), (3, twin))):
            at = 2 + 3 * k + j
            copies.append(remote(src, dst.at[slot], send.at[at], recv.at[at], peer))
    for copy in copies:
        copy.start()
    for copy in local:
        copy.wait()
    for copy in copies:
        copy.wait()


def entry(coords, rows, cols, tots):
    dma = pltpu.SemaphoreType.DMA
    return pl.pallas_call(
        functools.partial(entry_kernel, lax.axis_size("blk")),
        out_shape=(
            sds((3,) + coords.shape),
            sds((4,) + rows.shape, jnp.int32),
            sds((4,) + cols.shape, jnp.int32),
            sds((4,) + tots.shape, jnp.int32),
        ),
        in_specs=[VMEM] * 4,
        out_specs=(VMEM,) * 4,
        scratch_shapes=[dma((11,)), dma((11,)), dma((4,))],
        compiler_params=pltpu.CompilerParams(
            collective_id=0, has_side_effects=True, vmem_limit_bytes=2**21
        ),
        name="entry",
    )(coords, rows, cols, tots)


def exchange_kernel(n, own_ref, stat_ref, win_ref, all_ref, *sems):
    *wsems, ssend, srecv, lsem = sems
    half = lax.axis_index("sub")
    me = lax.axis_index("blk") * 2 + half
    twin = {"blk": lax.axis_index("blk"), "sub": 1 - half}
    up, down = peer_of(me, 2, n, "blk"), peer_of(me, -2, n, "blk")
    barrier = greet([peer_of(me, step, n, "blk") for step in range(1, n)])
    local = pltpu.make_async_copy(own_ref, win_ref.at[2], lsem)
    local.start()
    all_ref[me] = stat_ref[...]
    pl.semaphore_wait(barrier, n - 1)
    finish = ship(own_ref, win_ref, wsems, up, down, twin)
    stats = [
        remote(stat_ref, all_ref.at[me], ssend.at[step], srecv.at[step], peer_of(me, step, n, "blk"))
        for step in range(1, n)
    ]
    for copy in stats:
        copy.start()
    local.wait()
    finish()
    for copy in stats:
        copy.wait()


def exchange(own, stat, ident):
    n = lax.axis_size("blk") * 2
    dma = pltpu.SemaphoreType.DMA
    return pl.pallas_call(
        functools.partial(exchange_kernel, n),
        out_shape=(sds((5,) + own.shape), sds((n,) + stat.shape)),
        in_specs=[VMEM, VMEM],
        out_specs=(VMEM, VMEM),
        scratch_shapes=ship_sems(own) + [dma((n,)), dma((n,)), dma],
        compiler_params=pltpu.CompilerParams(
            collective_id=ident, has_side_effects=True, vmem_limit_bytes=2**22
        ),
        name=f"exchange{ident}",
    )(own, stat)


def share_kernel(n, own_ref, all_ref, send, recv, lsem):
    me = lax.axis_index("probe") * 2 + lax.axis_index("sub")

    def device(step):
        to = lax.rem(me + step, n)
        return {"probe": to // 2, "sub": lax.rem(to, 2)}

    barrier = pltpu.get_barrier_semaphore()
    for step in range(1, n):
        pl.semaphore_signal(barrier, inc=1, device_id=device(step), device_id_type=MESH)
    local = pltpu.make_async_copy(own_ref, all_ref.at[me], lsem)
    local.start()
    pl.semaphore_wait(barrier, n - 1)
    copies = []
    for step in range(1, n):
        copies.append(
            pltpu.make_async_remote_copy(
                src_ref=own_ref,
                dst_ref=all_ref.at[me],
                send_sem=send.at[step],
                recv_sem=recv.at[step],
                device_id=device(step),
                device_id_type=MESH,
            )
        )
    for copy in copies:
        copy.start()
    local.wait()
    for copy in copies:
        copy.wait()


def share(own, ident):
    n = lax.axis_size("probe") * 2
    return pl.pallas_call(
        functools.partial(share_kernel, n),
        out_shape=sds((n,) + own.shape),
        in_specs=[VMEM],
        out_specs=VMEM,
        scratch_shapes=[
            pltpu.SemaphoreType.DMA((n,)),
            pltpu.SemaphoreType.DMA((n,)),
            pltpu.SemaphoreType.DMA,
        ],
        compiler_params=pltpu.CompilerParams(collective_id=ident, has_side_effects=True, vmem_limit_bytes=2**21),
        name="share",
    )(own)


def block_of(ref, block, lo, hi):
    return ref[block // HB, lo:hi, (block % HB) * BL : (block % HB + 1) * BL]


def spread_points(x_ref, xb, half):
    for c in range(WB):
        at = c + HB * half
        flat = x_ref[at // SB, :, pl.ds(pl.multiple_of((at % SB) * BL, BL), BL)]
        cols = jnp.concatenate([flat, flat, flat[0:2]], axis=0).T
        for k in range(3):
            xb[c, k] = jnp.broadcast_to(cols[:, k : k + 1], (BL, BL))


def own_row(x_ref, half, a, k):
    return x_ref[1, k : k + 1, pl.ds(pl.multiple_of((a + HB * half) * BL, BL), BL)]


def local_stats(q, w, st_ref):
    square = jnp.sum(q * q, axis=1, keepdims=True)
    guess = jnp.sum(q * w, axis=1, keepdims=True) / jnp.maximum(square, TINY)
    rest = w - guess * q
    resid = jnp.sum(rest * rest, axis=1, keepdims=True)
    lane = lax.broadcasted_iota(jnp.int32, (q.shape[0], BL), 1)
    mixed = jnp.where(lane == 0, guess, jnp.where(lane == 1, resid, square))
    full = jnp.concatenate([mixed] * (BL // q.shape[0]), axis=0)
    st_ref[...] = full.T[0:8, :]


def alpha_beta(st_ref, ab_ref, n, probes, total_pts):
    guess = [st_ref[d, 0:1, :] for d in range(n)]
    square = [st_ref[d, 2:3, :] for d in range(n)]
    alpha = guess[0] * square[0]
    for d in range(1, n):
        alpha = alpha + guess[d] * square[d]
    alpha = alpha / total_pts
    resid = jnp.zeros_like(alpha)
    for d in range(n):
        gap = alpha - guess[d]
        resid = resid + (st_ref[d, 1:2, :] + gap * gap * square[d])
    beta = jnp.sqrt(resid / total_pts + EPSILON)
    row = lax.broadcasted_iota(jnp.int32, (8, BL), 0)
    ab = jnp.where(row == 0, alpha, beta)
    ab_ref[...] = ab
    cols = jnp.concatenate([ab] * 16, axis=0).T
    return cols[0:probes, 0:1], cols[0:probes, 1:2]


def split(value):
    high = value.astype(BF16)
    return high, (value - high.astype(F32)).astype(BF16)


def build_kernel(m_ref, raw_ref, wb_ref, ap_ref, np_ref, k_ref, dbuf, xb, x_ref, mult):
    half = lax.axis_index("sub")
    for slab in range(3):
        raw = raw_ref[slab]
        x_ref[slab] = (raw + WARP_GAIN * jnp.tanh(raw)) * (1.0 / SCALE)

    def fill(a, slot):
        at = slot
        for o in range(OFFS):
            times = m_ref[a * OFFS + o]
            wb_ref[at] = a + o
            mult[at] = times.astype(F32) * SIGNAL_VAR
            ap_ref[at // 2] = a
            at = at + (times > 0).astype(jnp.int32)
        wb_ref[at] = a + SB
        mult[at] = jnp.float32(0.0)
        ap_ref[at // 2] = a
        return slot + (at - slot + 1) // 2 * 2

    slots = lax.fori_loop(0, HB, fill, 0)
    used = slots // 2
    padded = (used + UNROLL - 1) // UNROLL * UNROLL

    def pad(i, _):
        ap_ref[i] = HB - 1
        for e in range(2):
            wb_ref[2 * i + e] = HB - 1 + SB
            mult[2 * i + e] = jnp.float32(0.0)
        return 0

    lax.fori_loop(used, padded, pad, 0)
    np_ref[0] = padded
    spread_points(x_ref, xb, half)

    def step(i, _):
        a = ap_ref[i]
        for e in range(2):
            c = wb_ref[2 * i + e]
            dist = None
            for k in range(3):
                differ = xb[c, k] - own_row(x_ref, half, a, k)
                dist = differ * differ if dist is None else dist + differ * differ
            taper = jnp.maximum(1.0 - dist, 0.0)
            weight = mult[2 * i + e] * jnp.exp2(dist * EXPO) * taper
            high, low = split(weight * taper)
            rows = pl.ds(e * BL, BL)
            k_ref[i, rows, 0:BL] = high
            k_ref[i, rows, BL : 2 * BL] = low
            dbuf[i, rows, :] = weight * (taper * SLOPE + 2.0)
        return 0

    lax.fori_loop(0, padded, step, 0)


def build(m, points):
    return pl.pallas_call(
        build_kernel,
        out_shape=(
            sds((2 * PAIRS + 8,), jnp.int32),
            sds((PAIRS + 8,), jnp.int32),
            sds((1,), jnp.int32),
            pltpu.VMEM((PAIRS, 2 * BL, 2 * BL), BF16),
            pltpu.VMEM((PAIRS, 2 * BL, BL), F32),
            pltpu.VMEM((WB, 3, BL, BL), F32),
            sds(points.shape),
        ),
        in_specs=[SMEM, VMEM],
        out_specs=(SMEM, SMEM, SMEM, VMEM, VMEM, VMEM, VMEM),
        scratch_shapes=[pltpu.SMEM((2 * PAIRS + 8,), F32)],
        compiler_params=pltpu.CompilerParams(vmem_limit_bytes=BUILD_VMEM),
        cost_estimate=pl.CostEstimate(flops=10**9, bytes_accessed=10**7, transcendentals=10**7),
        name="build",
    )(m, points)


def product(wb_ref, ap_ref, count, k_ref, vb, acc, probes):
    acc[...] = jnp.zeros_like(acc)

    def step(u, _):
        made = []
        for t in range(UNROLL):
            i = u * UNROLL + t
            left = jnp.concatenate([vb[wb_ref[2 * i]], vb[wb_ref[2 * i + 1]]], axis=1)
            both = jnp.dot(left, k_ref[i], preferred_element_type=F32)
            both = both[:, 0:BL] + both[:, BL : 2 * BL]
            if both.shape[0] > probes:
                both = both[0:probes] + both[probes:]
            made.append(both)
        for t in range(UNROLL):
            acc[ap_ref[u * UNROLL + t]] += made[t]
        return 0

    lax.fori_loop(0, count // UNROLL, step, 0)


def noise_row(noise_ref, a):
    at = (a + HB * lax.axis_index("sub")) * BL
    return noise_ref[0:1, pl.ds(pl.multiple_of(at, BL), BL)]


def first_kernel(
    wb_ref, ap_ref, np_ref, k_ref, own_ref, below_ref, above_ref, cross_ref, noise_ref, slopes_ref,
    w_ref, st_ref, q_ref, vb, acc,
):
    probes = w_ref.shape[0]
    half = lax.axis_index("sub")

    def place(part, values):
        q_ref[part] = values
        for c in range(HB):
            vb[part * HB + c] = values[:, c * BL : (c + 1) * BL].astype(BF16)

    def own(side):
        at = pl.multiple_of(side * HB * BL, HB * BL)
        return own_ref[:, pl.ds(at, HB * BL)].astype(F32)

    place(0, below_ref[...].astype(F32))
    place(2, own(half))
    place(4, above_ref[...].astype(F32))
    place(1 + 2 * half, cross_ref[...].astype(F32))
    place(3 - 2 * half, own(1 - half))
    product(wb_ref, ap_ref, np_ref[0], k_ref, vb, acc, probes)
    for a in range(HB):
        lanes = slice(a * BL, (a + 1) * BL)
        w_ref[:, lanes] = acc[a] + noise_row(noise_ref, a) * q_ref[2, :, lanes]
    local_stats(q_ref[2], w_ref[...], st_ref)


def first_apply(lists, tiles, slopes, own, below, above, cross, noise):
    probes = own.shape[0]
    return pl.pallas_call(
        first_kernel,
        out_shape=(sds((probes, HB * BL)), sds((8, BL)), sds((5, probes, HB * BL))),
        in_specs=[SMEM, SMEM, SMEM] + [VMEM] * 7,
        out_specs=(VMEM,) * 3,
        scratch_shapes=[
            pltpu.VMEM((WB, probes, BL), BF16),
            pltpu.VMEM((HB, probes, BL), F32),
        ],
        compiler_params=pltpu.CompilerParams(vmem_limit_bytes=APPLY_VMEM),
        name="first_apply",
    )(*lists, tiles, own, below, above, cross, noise, slopes)


def apply_kernel(
    total_pts, wb_ref, ap_ref, np_ref, k_ref, win_ref, old_ref, stat_ref, noise_ref, slopes_ref,
    w_ref, st_ref, q_ref, ab_ref, vb, acc,
):
    probes = win_ref.shape[1]
    alpha, beta = alpha_beta(stat_ref, ab_ref, stat_ref.shape[0], probes, total_pts)
    scale = 1.0 / beta
    for c in range(WB):
        q = (block_of(win_ref, c, 0, probes) - alpha * block_of(old_ref, c, 0, probes)) * scale
        q_ref[c // HB, :, (c % HB) * BL : (c % HB + 1) * BL] = q
        high, low = split(q)
        vb[c, 0:probes, :] = high
        vb[c, probes : 2 * probes, :] = low
    product(wb_ref, ap_ref, np_ref[0], k_ref, vb, acc, probes)
    for a in range(HB):
        lanes = slice(a * BL, (a + 1) * BL)
        w_ref[:, lanes] = (
            acc[a] + noise_row(noise_ref, a) * q_ref[2, :, lanes] - beta * old_ref[2, :, lanes]
        )
    local_stats(q_ref[2], w_ref[...], st_ref)


def apply(lists, tiles, slopes, window, old, stats, noise, total_pts):
    probes = window.shape[1]
    return pl.pallas_call(
        functools.partial(apply_kernel, total_pts),
        out_shape=(
            sds((probes, HB * BL)),
            sds((8, BL)),
            sds((5, probes, HB * BL)),
            sds((8, BL)),
        ),
        in_specs=[SMEM, SMEM, SMEM] + [VMEM] * 6,
        out_specs=(VMEM,) * 4,
        scratch_shapes=[
            pltpu.VMEM((WB, 2 * probes, BL), BF16),
            pltpu.VMEM((HB, probes, BL), F32),
        ],
        compiler_params=pltpu.CompilerParams(vmem_limit_bytes=APPLY_VMEM),
        name="apply",
    )(*lists, tiles, window, old, stats, noise, slopes)


def grad_kernel(
    total_pts, wb_ref, ap_ref, np_ref, dbuf, win_ref, old_ref, stat_ref, first_ref, x_ref, xb,
    ab0, ab1, last_ref, alphas_ref, betas_ref, g_ref, ab2, left_of, right_of, acc,
):
    half = lax.axis_index("sub")
    probes = win_ref.shape[1]

    alpha, beta = alpha_beta(stat_ref, ab2, stat_ref.shape[0], probes, total_pts)
    for it, ab in enumerate((ab0, ab1, ab2)):
        alphas_ref[it : it + 1, :] = ab[0:1, 0:probes]
        betas_ref[it : it + 1, :] = ab[1:2, 0:probes]
    scale = 1.0 / beta
    for c in range(WB):
        q = (block_of(win_ref, c, 0, probes) - alpha * block_of(old_ref, c, 0, probes)) * scale
        if c // HB in (1, 2, 3):
            part = c // HB + half - 2

            @pl.when((part >= 0) & (part < 2))
            def _(q=q, part=part, c=c):
                at = pl.multiple_of((part * HB + c % HB) * BL, BL)
                last_ref[:, pl.ds(at, BL)] = q

        high, low = split(q)
        sign = block_of(first_ref, c, 0, probes).astype(BF16)
        left_of[c] = jnp.concatenate([high, low, sign, sign], axis=0).T
        if c // HB == 2:
            right_of[c % HB] = jnp.concatenate([sign, sign, high, low], axis=0)
    acc[...] = jnp.zeros_like(acc)

    def step(u, _):
        made = []
        for t in range(2):
            i = 2 * u + t
            a = ap_ref[i]
            right = right_of[a]
            made.append(
                [
                    jnp.dot(left_of[wb_ref[2 * i + e]], right, preferred_element_type=F32)
                    for e in range(2)
                ]
            )
        for t in range(2):
            i = 2 * u + t
            a = ap_ref[i]
            sums = [None] * 3
            for e in range(2):
                c = wb_ref[2 * i + e]
                weight = made[t][e] * dbuf[i, pl.ds(e * BL, BL), :]
                for k in range(3):
                    term = weight * (xb[c, k] - own_row(x_ref, half, a, k))
                    term = jnp.sum(term.reshape(16, 8, BL), axis=0)
                    sums[k] = term if sums[k] is None else sums[k] + term
            for k in range(3):
                acc[a, k] += sums[k]
        return 0

    lax.fori_loop(0, np_ref[0] // 2, step, 0)
    g_ref[...] = jnp.zeros_like(g_ref)
    for a in range(HB):
        for k in range(3):
            g_ref[k : k + 1, a * BL : (a + 1) * BL] = jnp.sum(acc[a, k], axis=0, keepdims=True)


def grad(lists, slopes, window, old, stats, first, points, spread, ab0, ab1, total_pts):
    probes = window.shape[1]
    return pl.pallas_call(
        functools.partial(grad_kernel, total_pts),
        out_shape=(
            sds((probes, 2 * HB * BL)),
            sds((ITERS, probes)),
            sds((ITERS, probes)),
            sds((8, HB * BL)),
        ),
        in_specs=[SMEM, SMEM, SMEM] + [VMEM] * 9,
        out_specs=(VMEM,) * 4,
        scratch_shapes=[
            pltpu.VMEM((8, BL), F32),
            pltpu.VMEM((WB, BL, 4 * probes), BF16),
            pltpu.VMEM((HB, 4 * probes, BL), BF16),
            pltpu.VMEM((HB, 3, 8, BL), F32),
        ],
        compiler_params=pltpu.CompilerParams(vmem_limit_bytes=GRAD_VMEM),
        name="grad",
    )(*lists, slopes, window, old, stats, first, points, spread, ab0, ab1)


def multiplicity(rows, cols, tots, half, slots):
    spot = jnp.arange(slots, dtype=jnp.int32)[None, :]
    frame = jnp.array([0, 0, SB, SB], jnp.int32)[:, None]
    rows = rows.reshape(4, slots)
    offs = cols.reshape(4, slots) - rows
    live = spot < tots.reshape(4, 1)
    key = jnp.where(live, (rows + frame) * 32 + offs, -1).reshape(-1)
    out = SB + HB * half + jnp.arange(HB, dtype=jnp.int32)[:, None]
    off = jnp.arange(-SB, SB + 1, dtype=jnp.int32)[None, :]
    ahead = jnp.where(off >= 0, out * 32 + off, -2).reshape(-1)
    behind = jnp.where(off <= 0, (out + off) * 32 - off, -2).reshape(-1)
    hits = (ahead[:, None] == key).astype(jnp.int32) + (behind[:, None] == key)
    return jnp.sum(hits, axis=1)


def body(coords, noise_var, probe_signs, tile_rows, tile_cols, tile_count):
    half = lax.axis_index("sub")
    blk = lax.axis_size("blk")
    slab_pts = coords.shape[1]
    half_pts = slab_pts // 2
    probes = probe_signs.shape[0]
    total_pts = slab_pts * blk
    all_probes = probes * lax.axis_size("probe")
    slots = tile_rows.size
    signs = lax.dynamic_slice_in_dim(probe_signs, half * half_pts, half_pts, 1)
    pair = ("blk", "sub")
    every = [(b, h) for b in range(blk) for h in range(2)]

    def hop(step, flip):
        perm = [(2 * b + h, (b + step(h)) % blk * 2 + (1 - h if flip else h)) for b, h in every]
        return lax.ppermute(signs, pair, perm)

    below, above, cross = hop(lambda h: 1, 0), hop(lambda h: -1, 0), hop(lambda h: 2 * h - 1, 1)
    points, *lists = entry(coords, tile_rows.reshape(1, -1), tile_cols.reshape(1, -1), tile_count)
    noise = noise_var.reshape(1, -1)
    *index, tiles, slopes, spread, points = build(multiplicity(*lists, half, slots), points)
    work, stat, first = first_apply(index, tiles, slopes, probe_signs, below, above, cross, noise)
    old = first
    pairs = []
    for it in range(1, ITERS):
        window, stats = exchange(work, stat, it)
        work, stat, old, ab = apply(index, tiles, slopes, window, old, stats, noise, total_pts)
        pairs.append(ab)
    window, stats = exchange(work, stat, ITERS)
    last, alphas, betas, part = grad(
        index, slopes, window, old, stats, first, points, spread, *pairs, total_pts
    )
    parts = share(part, ITERS + 1)
    parts = jnp.sum(parts.reshape(-1, 2, 8, half_pts), axis=0)[:, 0:3]
    warp = jnp.tanh(coords)
    factor = (SCALE * 2.0 / (TAPER_SQ * all_probes)) * (1.0 + WARP_GAIN * (1.0 - warp * warp))
    coord_grad = factor * jnp.concatenate([parts[0], parts[1]], axis=1)
    return (alphas, betas, last, coord_grad)


def solution(mesh):
    return jax.shard_map(
        body,
        mesh=mesh,
        in_specs=(
            P(None, ("groups", "blk")),
            P(("groups", "blk")),
            P("probe", ("groups", "blk")),
            P(("groups", "blk"), "sub", None),
            P(("groups", "blk"), "sub", None),
            P(("groups", "blk"), "sub"),
        ),
        out_specs=(
            P(None, ("groups", "probe")),
            P(None, ("groups", "probe")),
            P("probe", ("groups", "blk")),
            P(None, ("groups", "blk")),
        ),
        check_vma=False,
    )
```

profile of v0, /device:TPU:5, one launch (start us, length us, event | category | flops | bytes accessed | tf_op | source)
XLA Modules:
  0.0 95.0 jit_solution(11668382028882930602)
XLA Ops:
  0.7 1.0 %constant_dynamic-slice_fusion = s32[32,1024]{1,0:T(8,128)S(1)} fusion(s32[32,2048]{1,0:T(8,128)} %own_ref.1, s32[]{:T(128)S(6)} %select_n.29), kind=kLoop, calls=%fused_computation.13 | loop fusion | bytes 262148 | tf_op jit(solution)/shard_map/dynamic_slice | solution.py:593
  1.6 1.9 %collective-permute-start.2 = (s32[32,1024]{1,0:T(8,128)S(1)}, s32[32,1024]{1,0:T(8,128)S(1)}, u32[]{:S(2)}, u32[]{:S(2)}) collective-permute-start(s32[32,1024]{1,0:T(8,128)S(1)} %constant_dynamic-slice_fusion), channel_id=1, source_target_pairs={{0,13},{1,4},{4,1},{5,8},{8,5},{9,12},{12,9},{13,0},{2,15},{3,6},{... | collective-permute-start | bytes 393224 | tf_op jit(solution)/shard_map/ppermute | solution.py:599
  3.5 2.0 %collective-permute-start.1 = (s32[32,1024]{1,0:T(8,128)S(1)}, s32[32,1024]{1,0:T(8,128)S(1)}, u32[]{:S(2)}, u32[]{:S(2)}) collective-permute-start(s32[32,1024]{1,0:T(8,128)S(1)} %constant_dynamic-slice_fusion), channel_id=1, source_target_pairs={{0,12},{1,13},{4,0},{5,1},{8,4},{9,5},{12,8},{13,9},{2,14},{3,15},... | collective-permute-start | bytes 393224 | tf_op jit(solution)/shard_map/ppermute | solution.py:599
  6.4 0.7 add.123
  7.6 0.8 copy-done.1
  8.4 0.7 copy-done.4
  9.0 0.7 copy-done.5
  9.7 7.8 %entry.1 = (f32[3,3,2048]{2,1,0:T(4,128)S(1)}, s32[4,1,96]{2,1,0:T(1,128)S(1)}, s32[4,1,96]{2,1,0:T(1,128)S(1)}, s32[4,1,1]{2,1,0:T(1,128)S(1)}) custom-call(f32[3,2048]{1,0:T(4,128)S(1)} %copy-done.1, s32[1,96]{1,0:T(1,128)S(1)} %bitcast.12, s32[1,96]{1,0:T(1,128)S(1)} %bitcast.13, s32[1,1]{1,0:T(1,128)S(6)} %copy.11.t_ref), custom_call_target="tpu_custom_call" | custom-call | tf_op jit(solution)/shard_map/entry/pallas_call | solution.py:137
  17.5 0.2 reduce
  17.7 0.1 lt.29
  17.8 0.5 broadcast.97
  18.3 0.7 reduce.8
  19.0 0.7 reduce.7
  19.9 0.3 add_reduce_fusion.m_ref
  20.1 10.7 %build.1 = (s32[280]{0:T(512)S(1)}, s32[144]{0:T(256)S(1)}, s32[1]{0:T(128)}, bf16[136,256,256]{2,1,0:T(8,128)(2,1)S(1)}, f32[136,256,128]{2,1,0:T(8,128)S(1)}, ...) custom-call(s32[264]{0:T(512)S(1)} %add_reduce_fusion.m_ref, f32[3,3,2048]{2,1,0:T(4,128)S(1)} %get-tuple-element.39.raw_ref), custom_call_target="tpu_custom_call" | custom-call | flops 1000000000 | bytes 10000000 | tf_op jit(solution)/shard_map/build/pallas_call | solution.py:351
  30.9 3.6 %first_apply.1 = (f32[32,1024]{1,0:T(8,128)S(1)}, f32[8,128]{1,0:T(8,128)S(1)}, f32[5,32,1024]{2,1,0:T(8,128)S(1)}) custom-call(s32[280]{0:T(512)S(1)} %get-tuple-element.40.wb_ref, s32[144]{0:T(256)S(1)} %get-tuple-element.41.ap_ref, s32[1]{0:T(128)} %get-tuple-element.42.np_ref, bf16[136,256,256]{2,1,0:T(8,128)(2,1)S(1)} %get-tuple-element.44.k_ref, ...), custom_call_target="tpu_custom_call" | custom-call | tf_op jit(solution)/shard_map/first_apply/pallas_call | solution.py:426
  34.5 12.8 %exchange1.1 = (f32[5,32,1024]{2,1,0:T(8,128)S(1)}, f32[8,8,128]{2,1,0:T(8,128)S(1)}) custom-call(f32[32,1024]{1,0:T(8,128)S(1)} %get-tuple-element.45.own_ref, f32[8,128]{1,0:T(8,128)S(1)} %get-tuple-element.46.stat_ref), custom_call_target="tpu_custom_call" | custom-call | tf_op jit(solution)/shard_map/exchange1/pallas_call | solution.py:182
  47.3 4.1 %apply.2 = (f32[32,1024]{1,0:T(8,128)S(1)}, f32[8,128]{1,0:T(8,128)S(1)}, f32[5,32,1024]{2,1,0:T(8,128)S(1)}, f32[8,128]{1,0:T(8,128)S(1)}) custom-call(s32[280]{0:T(512)S(1)} %get-tuple-element.40.wb_ref, s32[144]{0:T(256)S(1)} %get-tuple-element.41.ap_ref, s32[1]{0:T(128)} %get-tuple-element.42.np_ref, bf16[136,256,256]{2,1,0:T(8,128)(2,1)S(1)} %get-tuple-element.44.k_ref, ...), custom_call_target="tpu_custom_call" | custom-call | tf_op jit(solution)/shard_map/apply/pallas_call | solution.py:464
  51.4 12.7 %exchange2.1 = (f32[5,32,1024]{2,1,0:T(8,128)S(1)}, f32[8,8,128]{2,1,0:T(8,128)S(1)}) custom-call(f32[32,1024]{1,0:T(8,128)S(1)} %get-tuple-element.50.own_ref, f32[8,128]{1,0:T(8,128)S(1)} %get-tuple-element.51.stat_ref), custom_call_target="tpu_custom_call" | custom-call | tf_op jit(solution)/shard_map/exchange2/pallas_call | solution.py:182
  64.1 4.1 %apply.3 = (f32[32,1024]{1,0:T(8,128)S(1)}, f32[8,128]{1,0:T(8,128)S(1)}, f32[5,32,1024]{2,1,0:T(8,128)S(1)}, f32[8,128]{1,0:T(8,128)S(1)}) custom-call(s32[280]{0:T(512)S(1)} %get-tuple-element.40.wb_ref, s32[144]{0:T(256)S(1)} %get-tuple-element.41.ap_ref, s32[1]{0:T(128)} %get-tuple-element.42.np_ref, bf16[136,256,256]{2,1,0:T(8,128)(2,1)S(1)} %get-tuple-element.44.k_ref, ...), custom_call_target="tpu_custom_call" | custom-call | tf_op jit(solution)/shard_map/apply/pallas_call | solution.py:464
  68.1 12.6 %exchange3.1 = (f32[5,32,1024]{2,1,0:T(8,128)S(1)}, f32[8,8,128]{2,1,0:T(8,128)S(1)}) custom-call(f32[32,1024]{1,0:T(8,128)S(1)} %get-tuple-element.55.own_ref, f32[8,128]{1,0:T(8,128)S(1)} %get-tuple-element.56.stat_ref), custom_call_target="tpu_custom_call" | custom-call | tf_op jit(solution)/shard_map/exchange3/pallas_call | solution.py:182
  80.7 8.7 %grad.1 = (f32[32,2048]{1,0:T(8,128)}, f32[3,32]{1,0:T(4,128)}, f32[3,32]{1,0:T(4,128)}, f32[8,1024]{1,0:T(8,128)S(1)}) custom-call(s32[280]{0:T(512)S(1)} %get-tuple-element.40.wb_ref, s32[144]{0:T(256)S(1)} %get-tuple-element.41.ap_ref, s32[1]{0:T(128)} %get-tuple-element.42.np_ref, f32[136,256,128]{2,1,0:T(8,128)S(1)} %get-tuple-element.43.slopes_ref.dbuf, ...), custom_call_target="tpu_custom_call" | custom-call | tf_op jit(solution)/shard_map/grad/pallas_call | solution.py:548
  89.4 4.9 %share.1 = f32[4,8,1024]{2,1,0:T(8,128)S(1)} custom-call(f32[8,1024]{1,0:T(8,128)S(1)} %get-tuple-element.67.own_ref), custom_call_target="tpu_custom_call" | custom-call | tf_op jit(solution)/shard_map/share/pallas_call | solution.py:229
  94.4 0.6 maximum_multiply_fusion
  (35 shorter events, 1.0 us)
Async XLA Ops:
  0.6 30.3 %copy-start = (s32[32,2048]{1,0:T(8,128)S(1)}, s32[32,2048]{1,0:T(8,128)}, u32[]{:S(2)}) copy-start(s32[32,2048]{1,0:T(8,128)} %own_ref.1) | copy-start | bytes 786436
  0.6 30.3 %copy-start.3 = (f32[2048]{0:T(1024)S(1)}, f32[2048]{0:T(1024)}, u32[]{:S(2)}) copy-start(f32[2048]{0:T(1024)} %param.8) | copy-start | bytes 24580
  1.6 29.2 %collective-permute-start.2 = (s32[32,1024]{1,0:T(8,128)S(1)}, s32[32,1024]{1,0:T(8,128)S(1)}, u32[]{:S(2)}, u32[]{:S(2)}) collective-permute-start(s32[32,1024]{1,0:T(8,128)S(1)} %constant_dynamic-slice_fusion), channel_id=1, source_target_pairs={{0,13},{1,4},{4,1},{5,8},{8,5},{9,12},{12,9},{13,0},{2,15},{3,6},{... | collective-permute-start | bytes 393224 | tf_op jit(solution)/shard_map/ppermute | solution.py:599
  3.5 27.3 %collective-permute-start.1 = (s32[32,1024]{1,0:T(8,128)S(1)}, s32[32,1024]{1,0:T(8,128)S(1)}, u32[]{:S(2)}, u32[]{:S(2)}) collective-permute-start(s32[32,1024]{1,0:T(8,128)S(1)} %constant_dynamic-slice_fusion), channel_id=1, source_target_pairs={{0,12},{1,13},{4,0},{5,1},{8,4},{9,5},{12,8},{13,9},{2,14},{3,15},... | collective-permute-start | bytes 393224 | tf_op jit(solution)/shard_map/ppermute | solution.py:599
  5.5 25.4 %collective-permute-start = (s32[32,1024]{1,0:T(8,128)S(1)}, s32[32,1024]{1,0:T(8,128)S(1)}, u32[]{:S(2)}, u32[]{:S(2)}) collective-permute-start(s32[32,1024]{1,0:T(8,128)S(1)} %constant_dynamic-slice_fusion), channel_id=1, source_target_pairs={{0,4},{1,5},{4,8},{5,9},{8,12},{9,13},{12,0},{13,1},{2,6},{3,7},{6... | collective-permute-start | bytes 393224 | tf_op jit(solution)/shard_map/ppermute | solution.py:599
  7.6 0.8 copy-start.1
  8.4 0.7 copy-start.4
  9.0 0.7 copy-start.5
  68.1 26.2 %copy-start.2 = (f32[3,2048]{1,0:T(4,128)S(1)}, f32[3,2048]{1,0:T(4,128)}, u32[]{:S(2)}) copy-start(f32[3,2048]{1,0:T(4,128)} %x_ref.1) | copy-start | bytes 73732
where the time goes:
time: 94 us; the launch traced here: 95 us
  Pallas kernels  81.9 us (87%)
  local copies, waits for them, and re-layouts  5.22 us (6%)
  starting transfers between devices  3.89 us (4%)
  other arithmetic  2.51 us (3%)
  between operations  1.46 us (2%)
    pallas_call x3, Pallas kernels, exchange(): pl.pallas_call(functools.partial(exchange_kernel, n), out_shape=(sds((5,)...  38.1 us
    pallas_call x1, Pallas kernels, build(): pl.pallas_call(build_kernel, out_shape=(sds((2 * PAIRS + 8,), jnp.int32),...  10.7 us
    pallas_call x1, Pallas kernels, grad(): pl.pallas_call(functools.partial(grad_kernel, total_pts), out_shape=(sds(...  8.68 us
    pallas_call x2, Pallas kernels, apply(): pl.pallas_call(functools.partial(apply_kernel, total_pts), out_shape=(sds...  8.12 us
    pallas_call x1, Pallas kernels, entry(): pl.pallas_call(functools.partial(entry_kernel, lax.axis_size('blk')), out...  7.8 us
    pallas_call x1, Pallas kernels, share(): pl.pallas_call(functools.partial(share_kernel, n), out_shape=sds((n,) + o...  4.87 us
    ppermute x3, starting transfers between devices, hop(): return lax.ppermute(signs, pair, perm)  3.89 us
    pallas_call x1, Pallas kernels, first_apply(): pl.pallas_call(first_kernel, out_shape=(sds((probes, HB * BL)), sds((8, B...  3.61 us
  transfers between devices with their start and end apart: 3, of which 0 were waited for; matrix products, arithmetic and copies ran while one was open for 4% of the time, Pallas kernels for 20%

commit v1 on v0

v1 whole, which is shorter than its diff:
```python
import functools
import math

import jax
import jax.numpy as jnp
from jax import lax
from jax.experimental import pallas as pl
from jax.experimental.pallas import tpu as pltpu
from jax.sharding import PartitionSpec as P

ITERS = 3
SIGNAL_VAR = 0.1
LENGTH_SQ = 2.0
TAPER_SQ = 16.0
WARP_GAIN = 0.4
EPSILON = 1e-06

F32 = jnp.float32
BF16 = jnp.bfloat16
BL = 128
SB = 16
HB = 8
WB = 5 * HB
OFFS = 2 * SB + 1
SLOTS = 272
ZERO = SLOTS - 1
TINY = 1e-30
SCALE = math.sqrt(TAPER_SQ)
EXPO = -TAPER_SQ / (2.0 * LENGTH_SQ) / math.log(2.0)
SLOPE = TAPER_SQ / (2.0 * LENGTH_SQ)
BUILD_VMEM = 2**22
APPLY_VMEM = 8 * 2**20
GRAD_VMEM = 6 * 2**20
VMEM = pl.BlockSpec(memory_space=pltpu.VMEM)
SMEM = pl.BlockSpec(memory_space=pltpu.SMEM)
HBM = pl.BlockSpec(memory_space=pltpu.HBM)
MESH = pl.DeviceIdType.MESH


def sds(shape, dtype=F32):
    return jax.ShapeDtypeStruct(shape, dtype)


def peer_of(me, step, n, axis):
    to = lax.rem(me + step + n, n)
    return {axis: to // 2, "sub": lax.rem(to, 2)}


def greet(peers):
    barrier = pltpu.get_barrier_semaphore()
    for peer in peers:
        pl.semaphore_signal(barrier, inc=1, device_id=peer, device_id_type=MESH)
    return barrier


def remote(src, dst, send, recv, peer):
    return pltpu.make_async_remote_copy(
        src_ref=src, dst_ref=dst, send_sem=send, recv_sem=recv,
        device_id=peer, device_id_type=MESH,
    )


def ship(src, win_ref, sems, up, down, twin, direct):
    wsend, wrecv, fsend, frecv = sems
    half = lax.axis_index("sub")
    chunks = src.shape[0] // 8
    rows = [pl.ds(8 * c, 8) for c in range(chunks)]
    outs = []
    for c in range(chunks):
        outs.append(remote(src.at[rows[c]], win_ref.at[0, rows[c]], wsend.at[0, c], wrecv.at[0, c], up))
        outs.append(remote(src.at[rows[c]], win_ref.at[4, rows[c]], wsend.at[1, c], wrecv.at[1, c], down))
    for copy in outs:
        copy.start()
    own = None
    if direct:
        own = remote(src, win_ref.at[1 + 2 * half], fsend.at[chunks], frecv.at[chunks], twin)
        own.start()

    def hand(c):
        piece = win_ref.at[4 - 4 * half, rows[c]]
        return piece, remote(piece, win_ref.at[3 - 2 * half, rows[c]], fsend.at[c], frecv.at[c], twin)

    def wait_twin():
        if direct:
            own.wait()

    def forward():
        for c in range(chunks):
            piece, copy = hand(c)
            remote(piece, piece, wsend.at[0, c], wrecv.at[1 - half, c], twin).wait_recv()
            copy.start()

    def wait_direct():
        for c in range(chunks):
            other = win_ref.at[4 * half, rows[c]]
            remote(other, other, wsend.at[0, c], wrecv.at[half, c], twin).wait_recv()

    def wait_handed():
        for c in range(chunks):
            hand(c)[1].wait_recv()

    def drain():
        for copy in outs:
            copy.wait_send()
        for c in range(chunks):
            hand(c)[1].wait_send()

    return wait_twin, forward, wait_direct, wait_handed, drain


def ship_sems(chunks):
    dma = pltpu.SemaphoreType.DMA
    return [dma((2, chunks)), dma((2, chunks)), dma((chunks + 1,)), dma((chunks + 1,))]


def entry_kernel(n, x_ref, l_ref, win_ref, lists_ref, send, recv, lsem):
    blk, half = lax.axis_index("blk"), lax.axis_index("sub")
    above, below = lax.rem(blk + 1, n), lax.rem(blk + n - 1, n)
    up = {"blk": above, "sub": half}
    down = {"blk": below, "sub": half}
    cross = {"blk": above, "sub": 1 - half}
    under = {"blk": below, "sub": 1 - half}
    twin = {"blk": blk, "sub": 1 - half}
    barrier = greet((up, down, cross, under, twin))
    local = [
        pltpu.make_async_copy(x_ref, win_ref.at[1], lsem.at[0]),
        pltpu.make_async_copy(l_ref, lists_ref.at[2], lsem.at[1]),
    ]
    for copy in local:
        copy.start()
    pl.semaphore_wait(barrier, 5)
    copies = [
        remote(x_ref, win_ref.at[0], send.at[0], recv.at[0], up),
        remote(x_ref, win_ref.at[2], send.at[1], recv.at[1], down),
        remote(l_ref, lists_ref.at[1], send.at[2], recv.at[2], cross),
        remote(l_ref, lists_ref.at[0], send.at[3], recv.at[3], up),
        remote(l_ref, lists_ref.at[3], send.at[4], recv.at[4], twin),
    ]
    for copy in copies:
        copy.start()
    for copy in local:
        copy.wait()
    for copy in copies:
        copy.wait()


def entry(coords, listed):
    dma = pltpu.SemaphoreType.DMA
    return pl.pallas_call(
        functools.partial(entry_kernel, lax.axis_size("blk")),
        out_shape=(sds((3,) + coords.shape), sds((4,) + listed.shape, jnp.int32)),
        in_specs=[VMEM] * 2,
        out_specs=(VMEM,) * 2,
        scratch_shapes=[dma((5,)), dma((5,)), dma((2,))],
        compiler_params=pltpu.CompilerParams(
            collective_id=0, has_side_effects=True, vmem_limit_bytes=2**21
        ),
        name="entry",
    )(coords, listed)


def share_kernel(n, own_ref, all_ref, send, recv, lsem):
    me = lax.axis_index("probe") * 2 + lax.axis_index("sub")

    def device(step):
        to = lax.rem(me + step, n)
        return {"probe": to // 2, "sub": lax.rem(to, 2)}

    barrier = pltpu.get_barrier_semaphore()
    for step in range(1, n):
        pl.semaphore_signal(barrier, inc=1, device_id=device(step), device_id_type=MESH)
    local = pltpu.make_async_copy(own_ref, all_ref.at[me], lsem)
    local.start()
    pl.semaphore_wait(barrier, n - 1)
    copies = []
    for step in range(1, n):
        copies.append(
            pltpu.make_async_remote_copy(
                src_ref=own_ref,
                dst_ref=all_ref.at[me],
                send_sem=send.at[step],
                recv_sem=recv.at[step],
                device_id=device(step),
                device_id_type=MESH,
            )
        )
    for copy in copies:
        copy.start()
    local.wait()
    for copy in copies:
        copy.wait()


def share(own, ident):
    n = lax.axis_size("probe") * 2
    return pl.pallas_call(
        functools.partial(share_kernel, n),
        out_shape=sds((n,) + own.shape),
        in_specs=[VMEM],
        out_specs=VMEM,
        scratch_shapes=[
            pltpu.SemaphoreType.DMA((n,)),
            pltpu.SemaphoreType.DMA((n,)),
            pltpu.SemaphoreType.DMA,
        ],
        compiler_params=pltpu.CompilerParams(collective_id=ident, has_side_effects=True, vmem_limit_bytes=2**21),
        name="share",
    )(own)


def block_of(ref, block, lo, hi):
    return ref[block // HB, lo:hi, (block % HB) * BL : (block % HB + 1) * BL]


def spread_points(x_ref, xb, half):
    for c in range(WB):
        at = c + HB * half
        flat = x_ref[at // SB, :, pl.ds(pl.multiple_of((at % SB) * BL, BL), BL)]
        cols = jnp.concatenate([flat, flat, flat[0:2]], axis=0).T
        for k in range(3):
            xb[c, k] = jnp.broadcast_to(cols[:, k : k + 1], (BL, BL))


def own_row(x_ref, half, a, k):
    return x_ref[1, k : k + 1, pl.ds(pl.multiple_of((a + HB * half) * BL, BL), BL)]


def local_stats(q, w, st_ref):
    square = jnp.sum(q * q, axis=1, keepdims=True)
    guess = jnp.sum(q * w, axis=1, keepdims=True) / jnp.maximum(square, TINY)
    rest = w - guess * q
    resid = jnp.sum(rest * rest, axis=1, keepdims=True)
    lane = lax.broadcasted_iota(jnp.int32, (q.shape[0], BL), 1)
    mixed = jnp.where(lane == 0, guess, jnp.where(lane == 1, resid, square))
    full = jnp.concatenate([mixed] * (BL // q.shape[0]), axis=0)
    st_ref[...] = full.T[0:8, :]


def alpha_beta(st_ref, ab_ref, n, probes, total_pts):
    guess = [st_ref[d, 0:1, :] for d in range(n)]
    square = [st_ref[d, 2:3, :] for d in range(n)]
    alpha = guess[0] * square[0]
    for d in range(1, n):
        alpha = alpha + guess[d] * square[d]
    alpha = alpha / total_pts
    resid = jnp.zeros_like(alpha)
    for d in range(n):
        gap = alpha - guess[d]
        resid = resid + (st_ref[d, 1:2, :] + gap * gap * square[d])
    beta = jnp.sqrt(resid / total_pts + EPSILON)
    row = lax.broadcasted_iota(jnp.int32, (8, BL), 0)
    ab = jnp.where(row == 0, alpha, beta)
    ab_ref[...] = ab
    cols = jnp.concatenate([ab] * 16, axis=0).T
    return cols[0:probes, 0:1], cols[0:probes, 1:2]


def split(value):
    high = value.astype(BF16)
    return high, (value - high.astype(F32)).astype(BF16)


def multiplicity(lists_ref, slots, half):
    out = lax.broadcasted_iota(jnp.int32, (HB, BL), 0) + (SB + HB * half)
    off = lax.broadcasted_iota(jnp.int32, (BL, BL), 0) - SB
    spot = lax.broadcasted_iota(jnp.int32, (1, BL), 1)
    total = jnp.zeros((HB, BL), F32)
    for k in range(4):
        row = lists_ref[k, 0:1]
        step = lists_ref[k, 1:2] - row
        row = jnp.where(spot < lists_ref[k, 0:1, slots : slots + 1], row + (0 if k < 2 else SB), -4 * SB)
        for block, gap in ((row, step), (row + step, -step)):
            here = jnp.where(out == block, 1.0, 0.0).astype(BF16)
            there = jnp.where(off == gap, 1.0, 0.0).astype(BF16)
            total = total + lax.dot_general(
                here, there, (((1,), (1,)), ((), ())), preferred_element_type=F32
            )
    return total.astype(jnp.int32)


def build_kernel(
    slots, raw_ref, lists_ref, tab_ref, code_ref, np_ref, k_ref, dbuf, xb, x_ref,
    mv, ms, sem,
):
    half = lax.axis_index("sub")
    mv[...] = multiplicity(lists_ref, slots, half)
    move = pltpu.make_async_copy(mv, ms, sem)
    move.start()
    for slab in range(3):
        raw = raw_ref[slab]
        x_ref[slab] = (raw + WARP_GAIN * jnp.tanh(raw)) * (1.0 / SCALE)
    spread_points(x_ref, xb, half)
    k_ref[ZERO] = jnp.zeros((BL, 2 * BL), BF16)
    for a in range(HB):
        for w in list(range(a)) + list(range(a + OFFS, WB)):
            tab_ref[a * WB + w] = ZERO
    move.wait()

    def fill(a, at):
        for o in range(OFFS):
            live = (ms[a, o] > 0).astype(jnp.int32)
            code_ref[at] = a * 64 + o
            tab_ref[a * WB + a + o] = ZERO + live * (at - ZERO)
            at = at + live
        return at

    used = lax.fori_loop(0, HB, fill, 0)
    for t in range(4):
        code_ref[used + t] = SB
    padded = (used + 3) // 4 * 4
    np_ref[0] = padded

    def step(u, _):
        for e in range(2):
            i = 2 * u + e
            code = code_ref[i]
            a, o = code // 64, lax.rem(code, 64)
            times = (ms[a, o] * (i < used).astype(jnp.int32)).astype(F32) * SIGNAL_VAR
            dist = None
            for k in range(3):
                differ = xb[a + o, k] - own_row(x_ref, half, a, k)
                dist = differ * differ if dist is None else dist + differ * differ
            taper = jnp.maximum(1.0 - dist, 0.0)
            weight = times * jnp.exp2(dist * EXPO) * taper
            high, low = split(weight * taper)
            k_ref[i, :, 0:BL] = high
            k_ref[i, :, BL : 2 * BL] = low
            dbuf[i] = weight * (taper * SLOPE + 2.0)
        return 0

    lax.fori_loop(0, padded // 2, step, 0)


def build(points, lists, slots):
    return pl.pallas_call(
        functools.partial(build_kernel, slots),
        out_shape=(
            sds((HB * WB,), jnp.int32),
            sds((SLOTS,), jnp.int32),
            sds((1,), jnp.int32),
            pltpu.VMEM((SLOTS, BL, 2 * BL), BF16),
            pltpu.VMEM((SLOTS, BL, BL), F32),
            pltpu.VMEM((WB, 3, BL, BL), F32),
            sds(points.shape),
        ),
        in_specs=[VMEM] * 2,
        out_specs=(SMEM, SMEM, SMEM, VMEM, VMEM, VMEM, VMEM),
        scratch_shapes=[
            pltpu.VMEM((HB, BL), jnp.int32),
            pltpu.SMEM((HB, BL), jnp.int32),
            pltpu.SemaphoreType.DMA,
        ],
        compiler_params=pltpu.CompilerParams(vmem_limit_bytes=BUILD_VMEM),
        cost_estimate=pl.CostEstimate(flops=10**9, bytes_accessed=10**7, transcendentals=10**7),
        name="build",
    )(points, lists)


def noise_row(noise_ref, a):
    at = (a + HB * lax.axis_index("sub")) * BL
    return noise_ref[0:1, pl.ds(pl.multiple_of(at, BL), BL)]


def lanczos_kernel(
    n, total_pts, tab_ref, k_ref, slopes_ref, signs_ref, noise_ref,
    q_ref, first_ref, *refs,
):
    abs_ref, refs = refs[:ITERS], refs[ITERS:]
    sv, win, work, image, st, all_ref, vb, acc, lsem, ssend, srecv, *wsems = refs
    probes = first_ref.shape[1]
    blk, half = lax.axis_index("blk"), lax.axis_index("sub")
    me = blk * 2 + half
    twin = {"blk": blk, "sub": 1 - half}
    up, down = peer_of(me, 2, n, "blk"), peer_of(me, -2, n, "blk")
    pairs, handed, direct, passed = 3 - 2 * half, 1 + 2 * half, 4 * half, 4 - 4 * half
    pass_late = (half == 1) & (blk == 0) | (half == 0) & (blk == n // 2 - 1)
    barrier = greet([peer_of(me, step, n, "blk") for step in range(1, n)])
    wide = HB * BL

    def lanes(side):
        return pl.ds(pl.multiple_of(side * wide, wide), wide)

    mine = signs_ref.at[:, lanes(half)]
    local = [
        pltpu.make_async_copy(mine, sv.at[2], lsem.at[0]),
        pltpu.make_async_copy(signs_ref.at[:, lanes(1 - half)], sv.at[pairs], lsem.at[1]),
    ]
    for copy in local:
        copy.start()
    pl.semaphore_wait(barrier, n - 1)

    def part_product(p, rows):
        def step(u, _):
            made = []
            for t in range(2):
                at = (2 * u + t) * WB + p * HB
                right = jnp.concatenate([k_ref[tab_ref[at + w]] for w in range(HB)], axis=0)
                both = jnp.dot(vb[p, 0:rows], right, preferred_element_type=F32)
                both = both[:, 0:BL] + both[:, BL : 2 * BL]
                made.append(both if rows == probes else both[0:probes] + both[probes:])
            for t in range(2):
                acc[2 * u + t] += made[t]
            return 0

        lax.fori_loop(0, HB // 2, step, 0)

    def sweep(waits, load, rows):
        wait_twin, forward, wait_direct, wait_handed, drain = waits

        def part(p):
            load(p)
            part_product(p, rows)

        acc[...] = jnp.zeros_like(acc)
        part(2)
        wait_twin()
        part(pairs)

        @pl.when(jnp.logical_not(pass_late))
        def _():
            forward()
            part(passed)
            wait_direct()
            part(direct)
            wait_handed()
            part(handed)

        @pl.when(pass_late)
        def _():
            wait_direct()
            part(direct)
            wait_handed()
            part(handed)
            forward()
            part(passed)

        drain()

    def finish(it, beta):
        for a in range(HB):
            at = slice(a * BL, (a + 1) * BL)
            value = image[:, at] + noise_row(noise_ref, a) * q_ref[2, :, at]
            if it > 0:
                value = value - beta * work[ITERS, :, at]
            work[it, :, at] = value
        local_stats(q_ref[2], work[it], st.at[it])
        all_ref[it, me] = st[it]
        stats = [
            remote(st.at[it], all_ref.at[it, me], ssend.at[it, step], srecv.at[it, step], peer_of(me, step, n, "blk"))
            for step in range(1, n)
        ]
        for copy in stats:
            copy.start()
        waits = ship(work.at[it], win.at[it], wsems[4 + 4 * it : 8 + 4 * it], up, down, twin, True)
        return waits, stats

    def advance(it, stats):
        for copy in stats:
            copy.wait()
        return alpha_beta(all_ref.at[it], abs_ref[it], n, probes, total_pts)

    def window(it, p):
        return work[it] if p is None else win[it, p]

    waits = ship(mine, sv, wsems[0:4], up, down, twin, False)
    for copy in local:
        copy.wait()

    def load_signs(p):
        value = sv[p].astype(F32)
        first_ref[p] = value
        q_ref[p] = value
        vb[p, 0:probes] = value.astype(BF16)

    sweep(waits, load_signs, probes)
    for a in range(HB):
        image[:, a * BL : (a + 1) * BL] = acc[a]
    waits, stats = finish(0, None)
    for it in range(ITERS):
        win[it, 2] = work[it]
        if it < ITERS - 1:

            def load(p, it=it):
                high, low = split(win[it, p])
                vb[p, 0:probes] = high
                vb[p, probes : 2 * probes] = low

            sweep(waits, load, 2 * probes)
        else:
            wait_twin, forward, wait_direct, wait_handed, drain = waits
            wait_twin()
            forward()
            wait_direct()
            wait_handed()
            drain()
        alpha, beta = advance(it, stats)
        scale = 1.0 / beta
        work[ITERS] = q_ref[2]
        for p in range(5):
            q_ref[p] = (win[it, p] - alpha * q_ref[p]) * scale
        if it < ITERS - 1:
            for a in range(HB):
                at = slice(a * BL, (a + 1) * BL)
                image[:, at] = (acc[a] - alpha * image[:, at]) * scale
            waits, stats = finish(it + 1, beta)


def lanczos(tab, tiles, slopes, signs, noise, total_pts):
    probes = signs.shape[0]
    n = lax.axis_size("blk") * 2
    wide = HB * BL
    dma = pltpu.SemaphoreType.DMA
    sems = [sem for _ in range(ITERS + 1) for sem in ship_sems(probes // 8)]
    return pl.pallas_call(
        functools.partial(lanczos_kernel, n, total_pts),
        out_shape=(sds((5, probes, wide)),) * 2 + (sds((8, BL)),) * ITERS,
        in_specs=[SMEM, VMEM, VMEM, HBM, VMEM],
        out_specs=(VMEM,) * (2 + ITERS),
        scratch_shapes=[
            pltpu.VMEM((5, probes, wide), jnp.int32),
            pltpu.VMEM((ITERS, 5, probes, wide), F32),
            pltpu.VMEM((ITERS + 1, probes, wide), F32),
            pltpu.VMEM((probes, wide), F32),
            pltpu.VMEM((ITERS, 8, BL), F32),
            pltpu.VMEM((ITERS, n, 8, BL), F32),
            pltpu.VMEM((5, 2 * probes, wide), BF16),
            pltpu.VMEM((HB, probes, BL), F32),
            dma((2,)),
            dma((ITERS, n)),
            dma((ITERS, n)),
        ] + sems,
        compiler_params=pltpu.CompilerParams(
            collective_id=1, has_side_effects=True, vmem_limit_bytes=APPLY_VMEM
        ),
        name="lanczos",
    )(tab, tiles, slopes, signs, noise)


def grad_kernel(
    code_ref, np_ref, dbuf, win_ref, first_ref, x_ref, xb, ab0, ab1, ab2,
    last_ref, alphas_ref, betas_ref, g_ref, left_of, right_of, acc,
):
    half = lax.axis_index("sub")
    probes = win_ref.shape[1]
    for it, ab in enumerate((ab0, ab1, ab2)):
        alphas_ref[it : it + 1, :] = ab[0:1, 0:probes]
        betas_ref[it : it + 1, :] = ab[1:2, 0:probes]
    wide = HB * BL
    for side in range(2):
        last_ref[:, side * wide : (side + 1) * wide] = win_ref[2 + side - half]
    for c in range(WB):
        high, low = split(block_of(win_ref, c, 0, probes))
        sign = block_of(first_ref, c, 0, probes).astype(BF16)
        left_of[c] = jnp.concatenate([high, low, sign, sign], axis=0).T
        if c // HB == 2:
            right_of[c % HB] = jnp.concatenate([sign, sign, high, low], axis=0)
    acc[...] = jnp.zeros_like(acc)

    def step(u, _):
        codes = [code_ref[4 * u + t] for t in range(4)]
        rows = [code // 64 for code in codes]
        cols = [code // 64 + lax.rem(code, 64) for code in codes]
        made = [
            jnp.dot(left_of[c], right_of[a], preferred_element_type=F32) for a, c in zip(rows, cols)
        ]
        for t in range(4):
            a, c = rows[t], cols[t]
            weight = made[t] * dbuf[4 * u + t]
            for k in range(3):
                term = weight * (xb[c, k] - own_row(x_ref, half, a, k))
                acc[a, k] += jnp.sum(term.reshape(16, 8, BL), axis=0)
        return 0

    lax.fori_loop(0, np_ref[0] // 4, step, 0)
    g_ref[...] = jnp.zeros_like(g_ref)
    for a in range(HB):
        for k in range(3):
            g_ref[k : k + 1, a * BL : (a + 1) * BL] = jnp.sum(acc[a, k], axis=0, keepdims=True)


def grad(code, count, slopes, window, first, points, spread, pairs):
    probes = window.shape[1]
    return pl.pallas_call(
        grad_kernel,
        out_shape=(
            sds((probes, 2 * HB * BL)),
            sds((ITERS, probes)),
            sds((ITERS, probes)),
            sds((8, HB * BL)),
        ),
        in_specs=[SMEM, SMEM] + [VMEM] * 8,
        out_specs=(VMEM,) * 4,
        scratch_shapes=[
            pltpu.VMEM((WB, BL, 4 * probes), BF16),
            pltpu.VMEM((HB, 4 * probes, BL), BF16),
            pltpu.VMEM((HB, 3, 8, BL), F32),
        ],
        compiler_params=pltpu.CompilerParams(vmem_limit_bytes=GRAD_VMEM),
        name="grad",
    )(code, count, slopes, window, first, points, spread, *pairs)


def body(coords, noise_var, probe_signs, tile_rows, tile_cols, tile_count):
    blk = lax.axis_size("blk")
    slab_pts = coords.shape[1]
    half_pts = slab_pts // 2
    probes = probe_signs.shape[0]
    total_pts = slab_pts * blk
    all_probes = probes * lax.axis_size("probe")
    slots = tile_rows.size
    tail = jnp.broadcast_to(tile_count.reshape(1, 1), (1, BL - slots))
    listed = jnp.concatenate(
        [tile_rows.reshape(1, -1), tail, tile_cols.reshape(1, -1), tail], axis=1
    ).reshape(2, BL)
    points, lists = entry(coords, listed)
    noise = noise_var.reshape(1, -1)
    tab, code, count, tiles, slopes, spread, points = build(points, lists, slots)
    window, first, *pairs = lanczos(tab, tiles, slopes, probe_signs, noise, total_pts)
    last, alphas, betas, part = grad(code, count, slopes, window, first, points, spread, pairs)
    parts = share(part, 2)
    parts = jnp.sum(parts.reshape(-1, 2, 8, half_pts), axis=0)[:, 0:3]
    warp = jnp.tanh(coords)
    factor = (SCALE * 2.0 / (TAPER_SQ * all_probes)) * (1.0 + WARP_GAIN * (1.0 - warp * warp))
    coord_grad = factor * jnp.concatenate([parts[0], parts[1]], axis=1)
    return (alphas, betas, last, coord_grad)


def solution(mesh):
    return jax.shard_map(
        body,
        mesh=mesh,
        in_specs=(
            P(None, ("groups", "blk")),
            P(("groups", "blk")),
            P("probe", ("groups", "blk")),
            P(("groups", "blk"), "sub", None),
            P(("groups", "blk"), "sub", None),
            P(("groups", "blk"), "sub"),
        ),
        out_specs=(
            P(None, ("groups", "probe")),
            P(None, ("groups", "probe")),
            P("probe", ("groups", "blk")),
            P(None, ("groups", "blk")),
        ),
        check_vma=False,
    )
```

time: 94 us -> 83.2 us (0.89); the launches traced: 95 us -> 83 us
  local copies, waits for them, and re-layouts: 5.22 us -> 0.78 us
  starting transfers between devices: 3.89 us -> 0 us
  Pallas kernels: 81.9 us -> 79.4 us
  other arithmetic: 2.51 us -> 1.4 us
    ppermute x3 -> x0, starting transfers between devices: 3.89 us -> none  [hop(): return lax.ppermute(signs, pair, perm)]
    pallas_call x3 -> x0, other arithmetic: 1.49 us -> none  [entry(): pl.pallas_call(functools.partial(entry_kernel, lax.axis_size('blk')), out...]
    unnamed x12 -> x8, local copies, waits for them, and re-layouts: 2.09 us -> 0.77 us
    pallas_call x1, Pallas kernels: 7.8 us -> 6.55 us  [entry(): pl.pallas_call(functools.partial(entry_kernel, lax.axis_size('blk')), out...]
    add x8 -> x0, local copies, waits for them, and re-layouts: 1.2 us -> none  [the longest x2 0.81 us: multiplicity(): key = jnp.where(live, (rows + frame) * 32 + offs, -1).reshape(-1)]
    pallas_call x1, Pallas kernels: 4.87 us -> 3.9 us  [share(): pl.pallas_call(functools.partial(share_kernel, n), out_shape=sds((n,) + o...]
    dynamic_slice x1 -> x0, local copies, waits for them, and re-layouts: 0.96 us -> none  [body(): signs = lax.dynamic_slice_in_dim(probe_signs, half * half_pts, half_pts, 1)]
    pallas_call x8 -> x3, Pallas kernels: 69.2 us -> 68.9 us  [the longest x1 46.7 us: lanczos(): pl.pallas_call(functools.partial(lanczos_kernel, n, total_pts), out_shape...]
  transfers between devices with their start and end apart: 3 -> 0, of which waited for: 0 -> 0; matrix products, arithmetic and copies ran while one was open for 4% -> 0% of each run, Pallas kernels for 20% -> 0%
where the time goes in v1:
time: 83.2 us; the launch traced here: 83 us
  Pallas kernels  79.4 us (95%)
  between operations  1.42 us (2%)
  other arithmetic  1.4 us (2%)
    pallas_call x1, Pallas kernels, lanczos(): pl.pallas_call(functools.partial(lanczos_kernel, n, total_pts), out_shape...  46.7 us
    pallas_call x1, Pallas kernels, build(): pl.pallas_call(functools.partial(build_kernel, slots), out_shape=(sds((HB...  12.1 us
    pallas_call x1, Pallas kernels, grad(): pl.pallas_call(grad_kernel, out_shape=(sds((probes, 2 * HB * BL)), sds((I...  10.2 us
    pallas_call x1, Pallas kernels, entry(): pl.pallas_call(functools.partial(entry_kernel, lax.axis_size('blk')), out...  6.55 us
    pallas_call x1, Pallas kernels, share(): pl.pallas_call(functools.partial(share_kernel, n), out_shape=sds((n,) + o...  3.9 us

profile of v1, /device:TPU:5, one launch (start us, length us, event | category | flops | bytes accessed | tf_op | source)
XLA Modules:
  0.0 83.0 jit_solution(9177008134677984360)
XLA Ops:
  0.6 0.0 copy-start
  1.3 0.7 pad_add_fusion
  2.1 0.0 copy-start.1
  2.1 0.8 copy-done.1
  2.8 0.0 copy-start.3
  2.9 6.5 %entry.1 = (f32[3,3,2048]{2,1,0:T(4,128)S(1)}, s32[4,2,128]{2,1,0:T(2,128)S(1)}) custom-call(f32[3,2048]{1,0:T(4,128)S(1)} %copy-done.1, s32[2,128]{1,0:T(2,128)S(1)} %bitcast.13), custom_call_target="tpu_custom_call" | custom-call | tf_op jit(solution)/shard_map/entry/pallas_call | solution.py:149
  9.4 12.1 %build.1 = (s32[320]{0:T(512)S(1)}, s32[272]{0:T(512)S(1)}, s32[1]{0:T(128)}, bf16[272,128,256]{2,1,0:T(8,128)(2,1)S(1)}, f32[272,128,128]{2,1,0:T(8,128)S(1)}, ...) custom-call(f32[3,3,2048]{2,1,0:T(4,128)S(1)} %get-tuple-element.22.raw_ref, ...), custom_call_target="tpu_custom_call" | custom-call | flops 1000000000 | bytes 10000000 | tf_op jit(solution)/shard_map/build/pallas_call | solution.py:335
  21.5 0.0 copy-done
  21.5 0.0 copy-done.3
  21.5 46.7 %lanczos.1 = (f32[5,32,1024]{2,1,0:T(8,128)S(1)}, f32[5,32,1024]{2,1,0:T(8,128)S(1)}, f32[8,128]{1,0:T(8,128)S(1)}, f32[8,128]{1,0:T(8,128)S(1)}, f32[8,128]{1,0:T(8,128)S(1)}) custom-call(s32[320]{0:T(512)S(1)} %get-tuple-element.27.tab_ref, bf16[272,128,256]{2,1,0:T(8,128)(2,1)S(1)} %get-tuple-element.28.k_ref, ...), custom_call_target="tpu_custom_call" | custom-call | tf_op jit(solution)/shard_map/lanczos/pallas_call | solution.py:514
  68.2 0.0 copy-start.2
  68.2 10.2 %grad.1 = (f32[32,2048]{1,0:T(8,128)}, f32[3,32]{1,0:T(4,128)}, f32[3,32]{1,0:T(4,128)}, f32[8,1024]{1,0:T(8,128)S(1)}) custom-call(s32[272]{0:T(512)S(1)} %get-tuple-element.24.code_ref, s32[1]{0:T(128)} %get-tuple-element.25.np_ref, f32[272,128,128]{2,1,0:T(8,128)S(1)} %get-tuple-element.26.slopes_ref.dbuf, f32[5,32,1024]{2,1,0:T(8,128)S(1)} %get-tuple-element.29.win_ref, ...), custom_call_target="tpu_custom_call" | custom-call | tf_op jit(solution)/shard_map/grad/pallas_call | solution.py:583
  78.4 3.9 %share.1 = f32[4,8,1024]{2,1,0:T(8,128)S(1)} custom-call(f32[8,1024]{1,0:T(8,128)S(1)} %get-tuple-element.39.own_ref), custom_call_target="tpu_custom_call" | custom-call | tf_op jit(solution)/shard_map/share/pallas_call | solution.py:196
  82.3 0.0 copy-done.2
  82.3 0.6 maximum_multiply_fusion
  (3 shorter events, 0.0 us)
Async XLA Ops:
  0.6 20.9 %copy-start = (s32[32,2048]{1,0:T(8,128)S(1)}, s32[32,2048]{1,0:T(8,128)}, u32[]{:S(2)}) copy-start(s32[32,2048]{1,0:T(8,128)} %signs_ref.1) | copy-start | bytes 786436
  2.1 0.8 copy-start.1
  2.8 18.7 %copy-start.3 = (f32[2048]{0:T(1024)S(1)}, f32[2048]{0:T(1024)}, u32[]{:S(2)}) copy-start(f32[2048]{0:T(1024)} %param.7) | copy-start | bytes 24580
  68.2 14.1 %copy-start.2 = (f32[3,2048]{1,0:T(4,128)S(1)}, f32[3,2048]{1,0:T(4,128)}, u32[]{:S(2)}) copy-start(f32[3,2048]{1,0:T(4,128)} %x_ref.1) | copy-start | bytes 73732
